TPU v7x, 32 devices: a whole 2x2x4 slice. The times are simulated.
32 devices in a mesh: tilt: 2 (over y), row: 4 (over z), col: 2 (over x), probe: 2 (over core).
Axes of the slice: x: 2, y: 2, z: 4, core: 2. Of those that a mesh axis runs over, the one named last changes fastest.
Arguments:
- object_tiles: bfloat16 [4, 2, 1536, 768], P('tilt', None, 'row', 'col'), parts along dimension 0, may hold values from -1 to 1
- probe_modes: bfloat16 [8, 4, 128, 128], P('probe', 'tilt'), parts along dimension 1, may hold values from -6 to 6
- amplitudes: bfloat16 [4, 2, 4, 128, 128], P('row', 'col', 'tilt'), parts along dimension 2, may hold values from 0 to 4
- positions: int32 [4, 2, 4, 2], P('row', 'col', 'tilt'), parts along dimension 2, may hold values from 0 to 448, as said below
- counts: int32 [8, 2], P(('tilt', 'row'), 'col'), parts along dimension 0, may hold values from 1 to 2, as said below
- tilt_shift: float32 [4], P('tilt'), parts along dimension 0, may hold values from -6 to 6
Outputs:
- updated: float32 [4, 2, 1536, 768], P('tilt', None, 'row', 'col'), parts along dimension 0
There are 2 independent parts, one for each index of `tilt`. A program takes and returns all parts, laid end to end along the dimension named above; each array names one. Nothing has to cross between parts.
Inputs may be any that keep to these rules, and one draw needn't show every extreme that they name: Some tile has exactly 2 live positions; slots k >= counts of a tile are unused. `positions`: the extended frame's first pixel lies 96 pixels above and left of the tile's first core pixel.
All inputs are finite; a program needn't handle non-finite values.
Results may differ from a plain program's by a relative error of at most 0.0017.
Values may be sent and summed in bfloat16 or wider, within the bound.
No kernel may reach another device: no remote copies, remote signals or barrier semaphores. Data moves between devices by JAX's collectives and lax.ppermute only.
A program may use at most 64 MiB of HBM per device.

v0:
```python
import jax
import jax.numpy as jnp
from jax import lax
from jax.sharding import PartitionSpec as P

MARGIN = 96


FLOOR = 1.0
REGULAR = 1.0
CURVE = 1.5707963267948966
TWO_PI = 6.283185307179586


def extended_2(value, sides, width):
    for axis, dim in sides:
        size, length = (lax.axis_size(axis), value.shape[dim])
        up = [(i, (i + 1) % size) for i in range(size - 1)]
        down = [(j, i) for i, j in up]
        last = lax.slice_in_dim(value, length - width, length, axis=dim)
        leading = lax.slice_in_dim(value, 0, width, axis=dim)
        before = lax.ppermute(last, axis, up)
        after = lax.ppermute(leading, axis, down)
        value = jnp.concatenate([before, value, after], axis=dim)
    return value


def dft_tables(probe_side, tilt_shift):
    grid_index = jnp.arange(probe_side, dtype=jnp.int32)
    phase = (grid_index[:, None] * grid_index[None, :] % probe_side).astype(jnp.float32) * (
        TWO_PI / probe_side
    )
    scale = 1.0 / jnp.sqrt(jnp.float32(probe_side))
    centred = ((grid_index + probe_side // 2) % probe_side - probe_side // 2).astype(jnp.float32)
    chirp = (
        CURVE
        * (centred[:, None] * centred[:, None] + centred[None, :] * centred[None, :])
        / probe_side
        + TWO_PI
        * (tilt_shift[0] * centred[:, None] + tilt_shift[1] * centred[None, :])
        / probe_side
    )
    return (jnp.cos(phase) * scale, jnp.sin(phase) * scale, jnp.cos(chirp), jnp.sin(chirp))


def dft_pair(real_in, imag_in, table_real, table_imag):
    highest = lax.Precision.HIGHEST
    half_real = jnp.einsum("jk,mkl->mjl", table_real, real_in, precision=highest) - jnp.einsum(
        "jk,mkl->mjl", table_imag, imag_in, precision=highest
    )
    half_imag = jnp.einsum("jk,mkl->mjl", table_real, imag_in, precision=highest) + jnp.einsum(
        "jk,mkl->mjl", table_imag, real_in, precision=highest
    )
    out_real = jnp.einsum("mjl,lk->mjk", half_real, table_real, precision=highest) - jnp.einsum(
        "mjl,lk->mjk", half_imag, table_imag, precision=highest
    )
    out_imag = jnp.einsum("mjl,lk->mjk", half_real, table_imag, precision=highest) + jnp.einsum(
        "mjl,lk->mjk", half_imag, table_real, precision=highest
    )
    return (out_real, out_imag)


def fold_rows(gradient):
    sent = jnp.concatenate([gradient[:, :, :MARGIN], gradient[:, :, -MARGIN:]], axis=2)
    arrived = extended_2(sent.astype(jnp.bfloat16), (("row", 2),), MARGIN).astype(sent.dtype)
    inner = gradient[:, :, MARGIN:-MARGIN]
    inner = inner.at[:, :, :MARGIN].add(arrived[:, :, :MARGIN])
    return inner.at[:, :, -MARGIN:].add(arrived[:, :, -MARGIN:])


def fold_cols(gradient):
    sent = jnp.concatenate([gradient[:, :, :, :MARGIN], gradient[:, :, :, -MARGIN:]], axis=3)
    arrived = extended_2(sent.astype(jnp.bfloat16), (("col", 3),), MARGIN).astype(sent.dtype)
    inner = gradient[:, :, :, MARGIN:-MARGIN]
    inner = inner.at[:, :, :, :MARGIN].add(arrived[:, :, :, :MARGIN])
    return inner.at[:, :, :, -MARGIN:].add(arrived[:, :, :, -MARGIN:])


def apply_step(start_object, summed):
    return start_object - summed[:, 0:2] / (summed[:, 2:3] + REGULAR)


def body(object_tiles, probe_modes, amplitudes, positions, counts, tilt_shift):
    probe_side = probe_modes.shape[2]
    extended = extended_2(object_tiles, (("row", 2), ("col", 3)), MARGIN).astype(jnp.float32)
    cos_part, sin_part, kernel_real, kernel_imag = dft_tables(probe_side, tilt_shift)
    probe_real = probe_modes[:, 0].astype(jnp.float32)
    probe_imag = probe_modes[:, 1].astype(jnp.float32)
    probe_power = jnp.sum(probe_real * probe_real + probe_imag * probe_imag, axis=0)
    live_count = counts[0, 0]

    def patch_of(slot_index):
        corner = positions[0, 0, slot_index]
        starts = (0, 0, corner[0], corner[1])
        return (starts, lax.dynamic_slice(extended, starts, (2, 2, probe_side, probe_side)))

    def forward(slot_index):
        starts, object_patch = patch_of(slot_index)
        one_real, one_imag = (object_patch[0, 0], object_patch[0, 1])
        two_real, two_imag = (object_patch[1, 0], object_patch[1, 1])
        entry_real = probe_real * one_real - probe_imag * one_imag
        entry_imag = probe_real * one_imag + probe_imag * one_real
        spec_real, spec_imag = dft_pair(entry_real, entry_imag, cos_part, -sin_part)
        moved_real = spec_real * kernel_real - spec_imag * kernel_imag
        moved_imag = spec_real * kernel_imag + spec_imag * kernel_real
        wave_real, wave_imag = dft_pair(moved_real, moved_imag, cos_part, sin_part)
        exit_real = wave_real * two_real - wave_imag * two_imag
        exit_imag = wave_real * two_imag + wave_imag * two_real
        far_real, far_imag = dft_pair(exit_real, exit_imag, cos_part, -sin_part)
        local_power = jnp.sum(far_real * far_real + far_imag * far_imag, axis=0)
        return (wave_real, wave_imag, far_real, far_imag, local_power)

    def backward(
        slot_index, gradient, weight, wave_real, wave_imag, far_real, far_imag, total_power
    ):
        starts, object_patch = patch_of(slot_index)
        two_real, two_imag = (object_patch[1, 0], object_patch[1, 1])
        modelled = jnp.sqrt(total_power)
        factor = 1.0 - amplitudes[0, 0, slot_index].astype(jnp.float32) / jnp.maximum(
            modelled, FLOOR
        )
        back_real, back_imag = dft_pair(far_real * factor, far_imag * factor, cos_part, sin_part)
        grad_two_real = jnp.sum(wave_real * back_real + wave_imag * back_imag, axis=0)
        grad_two_imag = jnp.sum(wave_real * back_imag - wave_imag * back_real, axis=0)
        light_two = jnp.sum(wave_real * wave_real + wave_imag * wave_imag, axis=0)
        pulled_real = two_real * back_real + two_imag * back_imag
        pulled_imag = two_real * back_imag - two_imag * back_real
        pulled_spec_real, pulled_spec_imag = dft_pair(pulled_real, pulled_imag, cos_part, -sin_part)
        unmoved_real = pulled_spec_real * kernel_real + pulled_spec_imag * kernel_imag
        unmoved_imag = pulled_spec_imag * kernel_real - pulled_spec_real * kernel_imag
        entry_back_real, entry_back_imag = dft_pair(unmoved_real, unmoved_imag, cos_part, sin_part)
        grad_one_real = jnp.sum(probe_real * entry_back_real + probe_imag * entry_back_imag, axis=0)
        grad_one_imag = jnp.sum(probe_real * entry_back_imag - probe_imag * entry_back_real, axis=0)
        update = jnp.stack(
            [
                jnp.stack([grad_one_real, grad_one_imag, probe_power]),
                jnp.stack([grad_two_real, grad_two_imag, light_two]),
            ]
        )
        current = lax.dynamic_slice(gradient, starts, update.shape)
        return lax.dynamic_update_slice(gradient, current + weight * update, starts)

    def padded_step(slot_index, running):
        wave_real, wave_imag, far_real, far_imag, local_power = forward(slot_index)
        total_power = lax.psum(local_power.astype(jnp.bfloat16), "probe").astype(jnp.float32)
        weight = (slot_index < live_count).astype(jnp.float32)
        return backward(
            slot_index, running, weight, wave_real, wave_imag, far_real, far_imag, total_power
        )

    zero_grad = jnp.zeros((2, 3, extended.shape[2], extended.shape[3]), jnp.float32)
    slot_total = amplitudes.shape[2]
    gradient = lax.fori_loop(0, slot_total, padded_step, zero_grad)
    folded = fold_cols(fold_rows(gradient))
    start_object = object_tiles.astype(jnp.float32)
    summed = lax.psum(folded.astype(jnp.bfloat16), "probe").astype(jnp.float32)
    return apply_step(start_object, summed)


def solution(mesh):
    return jax.shard_map(
        body,
        mesh=mesh,
        in_specs=(
            P("tilt", None, "row", "col"),
            P("probe", "tilt", None, None),
            P("row", "col", "tilt", None, None),
            P("row", "col", "tilt", None),
            P(("tilt", "row"), "col"),
            P("tilt"),
        ),
        out_specs=P("tilt", None, "row", "col"),
        check_vma=False,
    )
```

profile of v0, /device:TPU:13, one launch (start us, length us, event | category | flops | bytes accessed | tf_op | source)
XLA Modules:
  0.0 265.8 jit_solution(3827145421189606200)
XLA Ops:
  8.5 3.2 %collective-permute-start = (bf16[2,2,96,384]{2,3,1,0:T(8,128)(2,1)S(1)}, bf16[2,2,96,384]{2,3,1,0:T(8,128)(2,1)S(1)}, u32[]{:S(2)}, u32[]{:S(2)}) collective-permute-start(bf16[2,2,96,384]{2,3,1,0:T(8,128)(2,1)S(1)} %get-tuple-element.690), channel_id=1, source_target_pairs={{0,4},{4,8},{8,12},{1,5},{5,9},{9,13},{2,6},{6,10},{10,14},{3,7},{... | collective-permute-start | bytes 884744 | tf_op jit(solution)/shard_map/ppermute | solution.py:22
  15.7 4.7 %collective-permute-done = bf16[2,2,96,384]{2,3,1,0:T(8,128)(2,1)S(1)} collective-permute-done((bf16[2,2,96,384]{2,3,1,0:T(8,128)(2,1)S(1)}, bf16[2,2,96,384]{2,3,1,0:T(8,128)(2,1)S(1)}, u32[]{:S(2)}, u32[]{:S(2)}) %collective-permute-start) | collective-permute-done | bytes 294944 | tf_op jit(solution)/shard_map/ppermute | solution.py:22
  20.4 2.9 %collective-permute-done.1 = bf16[2,2,96,384]{2,3,1,0:T(8,128)(2,1)S(1)} collective-permute-done((bf16[2,2,96,384]{2,3,1,0:T(8,128)(2,1)S(1)}, bf16[2,2,96,384]{2,3,1,0:T(8,128)(2,1)S(1)}, u32[]{:S(2)}, u32[]{:S(2)}) %collective-permute-start.1) | collective-permute-done | bytes 294944 | tf_op jit(solution)/shard_map/ppermute | solution.py:23
  23.8 3.1 %collective-permute-start.2 = (bf16[2,2,576,96]{2,3,1,0:T(8,128)(2,1)S(1)}, bf16[2,2,576,96]{2,3,1,0:T(8,128)(2,1)S(1)}, u32[]{:S(2)}, u32[]{:S(2)}) collective-permute-start(bf16[2,2,576,96]{2,3,1,0:T(8,128)(2,1)S(1)} %get-tuple-element.688), channel_id=1, source_target_pairs={{0,2},{1,3},{4,6},{5,7},{8,10},{9,11},{12,14},{13,15},{16,18},{17,... | collective-permute-start | bytes 1327112 | tf_op jit(solution)/shard_map/ppermute | solution.py:22
  28.4 7.3 %collective-permute-done.2 = bf16[2,2,576,96]{2,3,1,0:T(8,128)(2,1)S(1)} collective-permute-done((bf16[2,2,576,96]{2,3,1,0:T(8,128)(2,1)S(1)}, bf16[2,2,576,96]{2,3,1,0:T(8,128)(2,1)S(1)}, u32[]{:S(2)}, u32[]{:S(2)}) %collective-permute-start.2) | collective-permute-done | bytes 442400 | tf_op jit(solution)/shard_map/ppermute | solution.py:22
  35.7 3.9 %collective-permute-done.3 = bf16[2,2,576,96]{2,3,1,0:T(8,128)(2,1)S(1)} collective-permute-done((bf16[2,2,576,96]{2,3,1,0:T(8,128)(2,1)S(1)}, bf16[2,2,576,96]{2,3,1,0:T(8,128)(2,1)S(1)}, u32[]{:S(2)}, u32[]{:S(2)}) %collective-permute-start.3) | collective-permute-done | bytes 442400 | tf_op jit(solution)/shard_map/ppermute | solution.py:23
  39.5 3.3 %maximum_convert_fusion = f32[2,2,576,576]{2,3,1,0:T(8,128)} fusion(bf16[2,2,576,96]{2,3,1,0:T(8,128)(2,1)S(1)} %collective-permute-done.3, bf16[2,2,96,384]{2,3,1,0:T(8,128)(2,1)S(1)} %collective-permute-done.1, bf16[2,2,384,384]{2,3,1,0:T(8,128)(2,1)S(1)} %copy.164, bf16[2,2,96,384]{2,3,1,0:T(8,128)(2,1)S(1)} %collective-permute-done, ...), kind=kLoop, calls=%fused_computation.402 | loop fusion | flops 13271040 | bytes 7962624 | tf_op jit(solution)/shard_map/convert_element_type | solution.py:85
  42.8 4.0 %broadcast_in_dim.8 = f32[2,3,576,576]{3,2,1,0:T(8,128)} broadcast(f32[]{:T(128)} %constant.190.clone.1), dimensions={} | broadcast | bytes 7962628 | tf_op jit(solution)/shard_map/broadcast_in_dim | solution.py:151
  46.8 116.0 %while.21 = (s32[]{:T(128)}, f32[2,3,576,576]{3,2,1,0:T(8,128)}, s32[1,1,2,2]{3,2,1,0:T(2,128)S(1)}, s32[]{:T(128)}, f32[2,2,576,576]{2,3,1,0:T(8,128)}, /*index...) while((s32[]{:T(128)}, f32[2,3,576,576]{3,2,1,0:T(8,128)}, ...), condition=%wide.region_9.10_spmd.clone.clone.clone, body=%wide.region_1.9_spmd.clone.clone.clone.sunk | while | flops 4851744768 | bytes 45647676 | solution.py:153
  72.4 6.4 %psum.24 = bf16[128,128]{1,0:T(8,128)(2,1)S(1)} all-reduce(bf16[128,128]{1,0:T(8,128)(2,1)S(1)} %get-tuple-element.797), channel_id=1, replica_groups=mesh['tilt'=2,'row'=4,'col'=2,'probe'=2] {'probe'}, use_global_device_ids=true, to_apply=%region_3.3 | all-reduce | flops 16384 | bytes 65536 | tf_op jit(solution)/shard_map/while/body/eval_jaxpr/psum | solution.py:145
  98.5 4.1 %dynamic_update_slice.12 = f32[2,3,576,576]{3,2,1,0:T(8,128)} dynamic-update-slice(f32[2,3,576,576]{3,2,1,0:T(8,128)} %get-tuple-element.824, f32[2,3,128,128]{3,2,1,0:T(8,128)S(1)} %fusion.627, s32[]{:T(128)} %constant.189.clone.1..sunk, s32[]{:T(128)} %constant.189.clone.1..sunk, s32[]{:T(128)S(6)} %select_n.448, s32[]{:T(128)S(6)} %select_n.449) | dynamic-update-slice | bytes 786436 | tf_op jit(solution)/shard_map/while/body/eval_jaxpr/dynamic_update_slice | solution.py:141
  128.3 3.6 %psum.24 = bf16[128,128]{1,0:T(8,128)(2,1)S(1)} all-reduce(bf16[128,128]{1,0:T(8,128)(2,1)S(1)} %get-tuple-element.797), channel_id=1, replica_groups=mesh['tilt'=2,'row'=4,'col'=2,'probe'=2] {'probe'}, use_global_device_ids=true, to_apply=%region_3.3 | all-reduce | flops 16384 | bytes 65536 | tf_op jit(solution)/shard_map/while/body/eval_jaxpr/psum | solution.py:145
  151.9 5.2 %dynamic_update_slice.12 = f32[2,3,576,576]{3,2,1,0:T(8,128)} dynamic-update-slice(f32[2,3,576,576]{3,2,1,0:T(8,128)} %get-tuple-element.824, f32[2,3,128,128]{3,2,1,0:T(8,128)S(1)} %fusion.627, s32[]{:T(128)} %constant.189.clone.1..sunk, s32[]{:T(128)} %constant.189.clone.1..sunk, s32[]{:T(128)S(6)} %select_n.448, s32[]{:T(128)S(6)} %select_n.449) | dynamic-update-slice | bytes 786436 | tf_op jit(solution)/shard_map/while/body/eval_jaxpr/dynamic_update_slice | solution.py:141
  162.8 4.1 %convert.15 = bf16[2,3,576,576]{3,2,1,0:T(8,128)(2,1)S(1)} convert(f32[2,3,576,576]{3,2,1,0:T(8,128)} %get-tuple-element.459) | non-fusion elementwise | flops 1990656 | bytes 11943936 | tf_op jit(solution)/shard_map/convert.9
  167.1 4.1 %collective-permute-start.4 = (bf16[2,3,96,576]{3,2,1,0:T(8,128)(2,1)S(1)}, bf16[2,3,96,576]{3,2,1,0:T(8,128)(2,1)S(1)}, u32[]{:S(2)}, u32[]{:S(2)}) collective-permute-start(bf16[2,3,96,576]{3,2,1,0:T(8,128)(2,1)S(1)} %get-tuple-element.684), channel_id=1, source_target_pairs={{0,4},{4,8},{8,12},{1,5},{5,9},{9,13},{2,6},{6,10},{10,14},{3,7},{... | collective-permute-start | bytes 1990664 | tf_op jit(solution)/shard_map/ppermute | solution.py:22
  173.6 13.2 %collective-permute-done.4 = bf16[2,3,96,576]{3,2,1,0:T(8,128)(2,1)S(1)} collective-permute-done((bf16[2,3,96,576]{3,2,1,0:T(8,128)(2,1)S(1)}, bf16[2,3,96,576]{3,2,1,0:T(8,128)(2,1)S(1)}, u32[]{:S(2)}, u32[]{:S(2)}) %collective-permute-start.4) | collective-permute-done | bytes 663584 | tf_op jit(solution)/shard_map/ppermute | solution.py:22
  186.8 3.7 %collective-permute-done.5 = bf16[2,3,96,576]{3,2,1,0:T(8,128)(2,1)S(1)} collective-permute-done((bf16[2,3,96,576]{3,2,1,0:T(8,128)(2,1)S(1)}, bf16[2,3,96,576]{3,2,1,0:T(8,128)(2,1)S(1)}, u32[]{:S(2)}, u32[]{:S(2)}) %collective-permute-start.5) | collective-permute-done | bytes 663584 | tf_op jit(solution)/shard_map/ppermute | solution.py:23
  195.8 4.0 %collective-permute-start.6 = (bf16[2,3,384,96]{2,3,1,0:T(8,128)(2,1)S(1)}, bf16[2,3,384,96]{2,3,1,0:T(8,128)(2,1)S(1)}, u32[]{:S(2)}, u32[]{:S(2)}) collective-permute-start(bf16[2,3,384,96]{2,3,1,0:T(8,128)(2,1)S(1)} %copy.170), channel_id=1, source_target_pairs={{0,2},{1,3},{4,6},{5,7},{8,10},{9,11},{12,14},{13,15},{16,18},{17,... | collective-permute-start | bytes 1327112 | tf_op jit(solution)/shard_map/ppermute | solution.py:22
  199.8 5.1 %slice.287 = f32[2,3,384,384]{3,2,1,0:T(8,128)} slice(f32[2,3,384,576]{3,2,1,0:T(8,128)} %copy-done), slice={[0:2], [0:3], [0:384], [96:480]} | slice | bytes 7077888 | tf_op jit(solution)/shard_map/slice | solution.py:74
  207.9 3.2 %convert_add_fusion.1 = f32[2,3,384,96]{3,2,1,0:T(8,128)} fusion(f32[2,3,384,576]{3,2,1,0:T(8,128)} %copy-done, bf16[2,3,384,96]{3,2,1,0:T(8,128)(2,1)S(1)} %copy.173, bf16[2,3,384,96]{3,2,1,0:T(8,128)(2,1)S(1)} %get-tuple-element.686, bf16[2,3,384,96]{3,2,1,0:T(8,128)(2,1)S(1)} %get-tuple-element.687, bf16[2,3,384,96]{3,2,1,0:T(8,128)(2,1)S(1)} %copy.172), kind=kLoop, calls=%fused_computation.412 | loop fusion | flops 1990656 | bytes 3538944 | tf_op jit(solution)/shard_map/add | solution.py:75
  211.1 6.4 %scatter-add.16 = f32[2,3,384,384]{3,2,1,0:T(8,128)} dynamic-update-slice(f32[2,3,384,384]{3,2,1,0:T(8,128)} %slice.287, f32[2,3,384,96]{3,2,1,0:T(8,128)} %convert_add_fusion.1, s32[]{:T(128)} %constant.189.clone.1, s32[]{:T(128)} %constant.189.clone.1, s32[]{:T(128)} %constant.189.clone.1, s32[]{:T(128)} %constant.189.clone.1) | dynamic-update-slice | bytes 1769476 | tf_op jit(solution)/shard_map/scatter-add | solution.py:75
  220.3 6.7 %scatter-add.19 = f32[2,3,384,384]{3,2,1,0:T(8,128)} dynamic-update-slice(f32[2,3,384,384]{3,2,1,0:T(8,128)} %scatter-add.16, f32[2,3,384,96]{3,2,1,0:T(8,128)} %slice_add_fusion.2, s32[]{:T(128)} %constant.189.clone.1, s32[]{:T(128)} %constant.189.clone.1, s32[]{:T(128)} %constant.189.clone.1, s32[]{:T(128)} %constant.198.clone.1) | dynamic-update-slice | bytes 1769476 | tf_op jit(solution)/shard_map/scatter-add | solution.py:76
  227.0 3.4 %convert_element_type.195 = bf16[2,3,384,384]{3,2,1,0:T(8,128)(2,1)} convert(f32[2,3,384,384]{3,2,1,0:T(8,128)} %scatter-add.19) | non-fusion elementwise | flops 884736 | bytes 5308416 | tf_op jit(solution)/shard_map/convert_element_type | solution.py:156
  230.4 23.6 %all-reduce.2.cloned.1.call-done = bf16[2,3,384,384]{3,2,1,0:T(8,128)(2,1)} async-done(((bf16[2,3,384,384]{3,2,1,0:T(8,128)(2,1)}), bf16[2,3,384,384]{3,2,1,0:T(8,128)(2,1)}) %all-reduce.2.cloned.1.call-update) | async-done | bytes 1769488 | tf_op jit(solution)/shard_map/psum | solution.py:156
  (167 shorter events, 106.7 us)
Async XLA Ops:
  6.5 7.3 %copy-start.4 = (f32[2]{0:T(128)S(1)}, f32[2]{0:T(128)}, u32[]{:S(2)}) copy-start(f32[2]{0:T(128)} %param.21) | copy-start | bytes 28
  6.5 247.5 %all-reduce.2.cloned.1.call-start = ((), (), s32[]{:S(2)}) async-start(), calls=%async_computation | async-start | bytes 3538944 | tf_op jit(solution)/shard_map/psum | solution.py:156
  8.5 11.9 %collective-permute-start = (bf16[2,2,96,384]{2,3,1,0:T(8,128)(2,1)S(1)}, bf16[2,2,96,384]{2,3,1,0:T(8,128)(2,1)S(1)}, u32[]{:S(2)}, u32[]{:S(2)}) collective-permute-start(bf16[2,2,96,384]{2,3,1,0:T(8,128)(2,1)S(1)} %get-tuple-element.690), channel_id=1, source_target_pairs={{0,4},{4,8},{8,12},{1,5},{5,9},{9,13},{2,6},{6,10},{10,14},{3,7},{... | collective-permute-start | bytes 884744 | tf_op jit(solution)/shard_map/ppermute | solution.py:22
  11.7 11.6 %collective-permute-start.1 = (bf16[2,2,96,384]{2,3,1,0:T(8,128)(2,1)S(1)}, bf16[2,2,96,384]{2,3,1,0:T(8,128)(2,1)S(1)}, u32[]{:S(2)}, u32[]{:S(2)}) collective-permute-start(bf16[2,2,96,384]{2,3,1,0:T(8,128)(2,1)S(1)} %get-tuple-element.691), channel_id=1, source_target_pairs={{4,0},{8,4},{12,8},{5,1},{9,5},{13,9},{6,2},{10,6},{14,10},{7,3},{... | collective-permute-start | bytes 884744 | tf_op jit(solution)/shard_map/ppermute | solution.py:23
  15.7 12.6 %copy-start.2 = (bf16[4,2,128,128]{3,2,1,0:T(8,128)(2,1)S(1)}, bf16[4,2,128,128]{3,2,1,0:T(8,128)(2,1)}, u32[]{:S(2)}) copy-start(bf16[4,2,128,128]{3,2,1,0:T(8,128)(2,1)} %param.17) | copy-start | bytes 786436
  23.8 11.9 %collective-permute-start.2 = (bf16[2,2,576,96]{2,3,1,0:T(8,128)(2,1)S(1)}, bf16[2,2,576,96]{2,3,1,0:T(8,128)(2,1)S(1)}, u32[]{:S(2)}, u32[]{:S(2)}) collective-permute-start(bf16[2,2,576,96]{2,3,1,0:T(8,128)(2,1)S(1)} %get-tuple-element.688), channel_id=1, source_target_pairs={{0,2},{1,3},{4,6},{5,7},{8,10},{9,11},{12,14},{13,15},{16,18},{17,... | collective-permute-start | bytes 1327112 | tf_op jit(solution)/shard_map/ppermute | solution.py:22
  27.0 12.6 %collective-permute-start.3 = (bf16[2,2,576,96]{2,3,1,0:T(8,128)(2,1)S(1)}, bf16[2,2,576,96]{2,3,1,0:T(8,128)(2,1)S(1)}, u32[]{:S(2)}, u32[]{:S(2)}) collective-permute-start(bf16[2,2,576,96]{2,3,1,0:T(8,128)(2,1)S(1)} %get-tuple-element.689), channel_id=1, source_target_pairs={{2,0},{3,1},{6,4},{7,5},{10,8},{11,9},{14,12},{15,13},{18,16},{19,... | collective-permute-start | bytes 1327112 | tf_op jit(solution)/shard_map/ppermute | solution.py:23
  42.8 4.0 %copy-start.3 = (bf16[1,1,2,128,128]{4,3,2,1,0:T(8,128)(2,1)S(1)}, bf16[1,1,2,128,128]{4,3,2,1,0:T(8,128)(2,1)}, u32[]{:S(2)}) copy-start(bf16[1,1,2,128,128]{4,3,2,1,0:T(8,128)(2,1)} %param.18) | copy-start | bytes 196612
  42.8 4.0 %copy-start.5 = (s32[1,1,2,2]{3,2,1,0:T(2,128)S(1)}, s32[1,1,2,2]{3,2,1,0:T(2,128)}, u32[]{:S(2)}) copy-start(s32[1,1,2,2]{3,2,1,0:T(2,128)} %param.19) | copy-start | bytes 52
  162.8 10.4 %slice-start = ((s8[8847360]{0:T(1024)(128)(4,1)}), s8[4194304]{0:T(1024)(128)(4,1)S(1)}, s32[]{:S(2)}) async-start(s8[8847360]{0:T(1024)(128)(4,1)} %bitcast.403), calls=%async_computation.1 | async-start | bytes 8388608
  162.8 10.4 %slice-start.1 = ((s8[8847360]{0:T(1024)(128)(4,1)}), s8[4194304]{0:T(1024)(128)(4,1)S(1)}, s32[]{:S(2)}) async-start(s8[8847360]{0:T(1024)(128)(4,1)} %bitcast.403), calls=%async_computation.2 | async-start | bytes 8388608
  162.8 10.4 %slice-start.2 = ((s8[8847360]{0:T(1024)(128)(4,1)}), s8[458752]{0:T(1024)(128)(4,1)S(1)}, s32[]{:S(2)}) async-start(s8[8847360]{0:T(1024)(128)(4,1)} %bitcast.403), calls=%async_computation.3 | async-start | bytes 917504
  167.1 19.7 %collective-permute-start.4 = (bf16[2,3,96,576]{3,2,1,0:T(8,128)(2,1)S(1)}, bf16[2,3,96,576]{3,2,1,0:T(8,128)(2,1)S(1)}, u32[]{:S(2)}, u32[]{:S(2)}) collective-permute-start(bf16[2,3,96,576]{3,2,1,0:T(8,128)(2,1)S(1)} %get-tuple-element.684), channel_id=1, source_target_pairs={{0,4},{4,8},{8,12},{1,5},{5,9},{9,13},{2,6},{6,10},{10,14},{3,7},{... | collective-permute-start | bytes 1990664 | tf_op jit(solution)/shard_map/ppermute | solution.py:22
  171.2 19.3 %collective-permute-start.5 = (bf16[2,3,96,576]{3,2,1,0:T(8,128)(2,1)S(1)}, bf16[2,3,96,576]{3,2,1,0:T(8,128)(2,1)S(1)}, u32[]{:S(2)}, u32[]{:S(2)}) collective-permute-start(bf16[2,3,96,576]{3,2,1,0:T(8,128)(2,1)S(1)} %get-tuple-element.685), channel_id=1, source_target_pairs={{4,0},{8,4},{12,8},{5,1},{9,5},{13,9},{6,2},{10,6},{14,10},{7,3},{... | collective-permute-start | bytes 1990664 | tf_op jit(solution)/shard_map/ppermute | solution.py:23
  191.1 2.5 copy-start
  194.2 12.2 %collective-permute-start.7 = (bf16[2,3,384,96]{2,3,1,0:T(8,128)(2,1)S(1)}, bf16[2,3,384,96]{2,3,1,0:T(8,128)(2,1)S(1)}, u32[]{:S(2)}, u32[]{:S(2)}) collective-permute-start(bf16[2,3,384,96]{2,3,1,0:T(8,128)(2,1)S(1)} %copy.171), channel_id=1, source_target_pairs={{2,0},{3,1},{6,4},{7,5},{10,8},{11,9},{14,12},{15,13},{18,16},{19,... | collective-permute-start | bytes 1327112 | tf_op jit(solution)/shard_map/ppermute | solution.py:23
  195.8 11.8 %collective-permute-start.6 = (bf16[2,3,384,96]{2,3,1,0:T(8,128)(2,1)S(1)}, bf16[2,3,384,96]{2,3,1,0:T(8,128)(2,1)S(1)}, u32[]{:S(2)}, u32[]{:S(2)}) collective-permute-start(bf16[2,3,384,96]{2,3,1,0:T(8,128)(2,1)S(1)} %copy.170), channel_id=1, source_target_pairs={{0,2},{1,3},{4,6},{5,7},{8,10},{9,11},{12,14},{13,15},{16,18},{17,... | collective-permute-start | bytes 1327112 | tf_op jit(solution)/shard_map/ppermute | solution.py:22
  255.8 1.3 copy-start.1
Sparse Core Ops, SparseCore 0:
  230.6 23.4 all-reduce.1
where the time goes:
time: 271 us; the launch traced here: 266 us
  matrix products  72.9 us (27%)
  waiting for transfers between devices  61.6 us (23%)
  local copies, waits for them, and re-layouts  44.2 us (16%)
  other arithmetic  26.4 us (10%)
  starting transfers between devices  21.1 us (8%)
  loops' own time  15.7 us (6%)
  between operations  13.9 us (5%)
  blocking collectives  9.98 us (4%)
    ppermute x4, waiting for transfers between devices, extended_2(): before = lax.ppermute(last, axis, up)  26.1 us
    psum x1, waiting for transfers between devices, body(): summed = lax.psum(folded.astype(jnp.bfloat16), 'probe').astype(jnp.float32)  23.6 us
    another operation x1, loops' own time, body(): gradient = lax.fori_loop(0, slot_total, padded_step, zero_grad)  15.7 us
    ppermute x4, starting transfers between devices, extended_2(): before = lax.ppermute(last, axis, up)  14.5 us
    ppermute x4, waiting for transfers between devices, extended_2(): after = lax.ppermute(leading, axis, down)  11.9 us
    psum x2, blocking collectives, padded_step(): lax.psum(local_power.astype(jnp.bfloat16), 'probe').astype(jnp.float32)  9.98 us
    dot_general x12, matrix products, dft_pair(): jnp.einsum('mjl,lk->mjk', half_real, table_imag, precision=highest)  9.41 us
    dot_general x12, matrix products, dft_pair(): jnp.einsum('mjl,lk->mjk', half_imag, table_real, precision=highest)  9.4 us
  transfers between devices with their start and end apart: 9, of which 9 were waited for; matrix products, arithmetic and copies ran while one was open for 3% of the time, Pallas kernels for 0%

commit v1 on v0

v1 whole, which is shorter than its diff:
```python
import functools

import jax
import jax.numpy as jnp
import numpy as np
from jax import lax
from jax.experimental import pallas as pl
from jax.experimental.pallas import tpu as pltpu
from jax.sharding import PartitionSpec as P

MARGIN = 96
FLOOR = 1.0
REGULAR = 1.0
LANES = 128
TAIL = 16
BF = jnp.bfloat16
F32 = jnp.float32
VMEM = pl.BlockSpec(memory_space=pltpu.VMEM)
SMEM = pl.BlockSpec(memory_space=pltpu.SMEM)


def partner(index, phase, size):
    other = (index ^ 1) if phase == 0 else ((index + 1) ^ 1) - 1
    return other if 0 <= other < size else None


def phases_of(size):
    return [ph for ph in (0, 1) if any(partner(i, ph, size) is not None for i in range(size))]


def swap_pairs(sizes, row_phase, col_phase):
    rows, cols, cores = sizes
    pairs = []
    for r in range(rows):
        for c in range(cols):
            r2 = r if row_phase is None else partner(r, row_phase, rows)
            c2 = c if col_phase is None else partner(c, col_phase, cols)
            if r2 is None or c2 is None:
                continue
            for k in range(cores):
                pairs.append(((r * cols + c) * cores + k, (r2 * cols + c2) * cores + k))
    return pairs


def is_after(axis, phase):
    index = lax.axis_index(axis)
    return jnp.where(lax.rem(index, 2) == phase, 1, 0).astype(jnp.int32)


def onehot(shape, fn):
    i = lax.broadcasted_iota(jnp.int32, shape, 0)
    j = lax.broadcasted_iota(jnp.int32, shape, 1)
    return jnp.where(fn(i, j), 1.0, 0.0).astype(BF)


def dot(a, b):
    return jnp.dot(a, b, preferred_element_type=F32)


def split(x):
    hi = x.astype(BF)
    return hi, (x - hi.astype(F32)).astype(BF)


def prep_kernel(plan, obj_ref, *outs):
    planes, side, _ = obj_ref.shape
    m = MARGIN
    edge = -(-m // LANES) * LANES
    z_refs, x_refs, d_refs = outs[: len(plan.rows)], outs[len(plan.rows) : len(plan.rows) + len(plan.cols)], outs[len(plan.rows) + len(plan.cols) :]
    starts = [pl.multiple_of(is_after("row", ph) * (side - m), 32) for ph in plan.rows]
    for z_ref, start in zip(z_refs, starts):
        for p in range(planes):
            z_ref[p * m : (p + 1) * m, :] = obj_ref[p, pl.ds(start, m), :]
    d_iter = iter(d_refs)
    for x_ref, pc in zip(x_refs, plan.cols):
        after = is_after("col", pc)
        lane0 = pl.multiple_of(after * (side - edge), LANES)
        offset = after * (edge - m)
        stack = jnp.concatenate([obj_ref[p, :, pl.ds(lane0, edge)] for p in range(planes)], axis=1)

        def pick(i, j):
            local, lane = i % edge - offset, j % m
            return (i // edge == j // m) & (local == lane)

        x_ref[...] = dot(stack, onehot((planes * edge, planes * m), pick)).astype(BF)
    for ph_start in starts:
        for x_ref in x_refs:
            next(d_iter)[...] = x_ref[pl.ds(ph_start, m), :]


def right_pack(re, im):
    return jnp.concatenate([jnp.concatenate([re, im], 1), jnp.concatenate([-im, re], 1)], 0)


def left_pack(re, im):
    return jnp.concatenate([jnp.concatenate([re, -im], 1), jnp.concatenate([im, re], 1)], 0)


def table_kernel(f_ref, h_ref, out_ref):
    n = f_ref.shape[1]
    fr, fi = f_ref[0], f_ref[1]

    def circulant(hr, hi):
        vr, vi = fr * hr + fi * hi, fr * hi - fi * hr
        a_hi, a_lo = split(left_pack(vr, vi))
        b_hi, b_lo = split(left_pack(fr, fi))
        return dot(a_hi, b_hi) + (dot(a_lo, b_hi) + dot(a_hi, b_lo)) + dot(a_lo, b_lo)

    def store(at, value):
        hi, lo = split(value)
        out_ref[2 * at] = hi
        out_ref[2 * at + 1] = lo

    h0r, h0i, h1r, h1i = (h_ref[k : k + 1, :] for k in range(4))
    left = circulant(h0r, h0i)
    left_adj = circulant(h0r, -h0i)
    across = circulant(h1r, h1i)
    rt = across[:n, :n].T
    it = across[n:, :n].T
    store(0, left)
    store(1, right_pack(rt, it))
    store(2, left_adj)
    store(3, right_pack(across[:n, :n], -across[n:, :n]))


def main_kernel(plan, *refs):
    refs = list(refs)
    pos_ref, cnt_ref, obj_ref = refs[:3]
    refs = refs[3:]
    n_row, n_col = len(plan.rows), len(plan.cols)
    z_in, refs = refs[:n_row], refs[n_row:]
    x_in, refs = refs[:n_col], refs[n_col:]
    d_in, refs = refs[: n_row * n_col], refs[n_row * n_col :]
    q_refs, refs = refs[: plan.cores], refs[plan.cores :]
    amp_ref, fpack_ref, prop_ref = refs[:3]
    refs = refs[3:]
    z_out, refs = refs[:n_row], refs[n_row:]
    x_out, refs = refs[:n_col], refs[n_col:]
    d_out, refs = refs[: n_row * n_col], refs[n_row * n_col :]
    g_out, wave_ref, far_ref, gsum_ref = refs

    planes, side, _ = obj_ref.shape
    n = amp_ref.shape[1]
    m = MARGIN
    slot = lax.axis_index("probe")
    a, b = pos_ref[slot, 0], pos_ref[slot, 1]
    live = slot < cnt_ref[0, 0]

    row0 = [is_after("row", ph) * (side + m) for ph in plan.rows]
    col0 = [is_after("col", ph) * (side + m) for ph in plan.cols]

    r_own = onehot((n, side), lambda i, j: j + m == a + i)
    r_strip = [onehot((n, m), lambda i, j, o=o: j + o == a + i) for o in row0]
    c_own = onehot((side, n), lambda i, j: i + m == b + j)

    def rows_of(own, strips):
        value = dot(r_own, own)
        for r, s in zip(r_strip, strips):
            value += dot(r, s)
        return value.astype(BF)

    packed = [
        rows_of(x_in[c][...], [d_in[ph * n_col + c][...] for ph in range(n_row)]) for c in range(n_col)
    ]
    window = []
    for p in range(planes):
        cut = rows_of(obj_ref[p], [z[p * m : (p + 1) * m, :] for z in z_in])
        value = dot(cut, c_own)
        for c in range(n_col):
            pick = onehot(
                (planes * m, n),
                lambda i, j, o=col0[c], p=p: (i >= p * m) & (i < (p + 1) * m) & (i - p * m + o == b + j),
            )
            value += dot(packed[c], pick)
        window.append(value)
    p1r, p1i, p2r, p2i = window

    f_hi, f_lo, fc_hi, fc_lo = (fpack_ref[k] for k in range(4))

    def rmul(x, t_hi, t_lo):
        hi, lo = split(x)
        return dot(hi, t_hi) + (dot(lo, t_hi) + dot(hi, t_lo))

    def lmul(t_hi, t_lo, x):
        hi, lo = split(x)
        return dot(t_hi, hi) + (dot(t_hi, lo) + dot(t_lo, hi))

    def two_sided(parts, left, right):
        x = jnp.concatenate([jnp.concatenate(p, 1) for p in parts], 0)
        y = rmul(x, *right)
        k = len(parts)
        z = jnp.concatenate(
            [
                jnp.concatenate([y[i * n : (i + 1) * n, :n] for i in range(k)], 1),
                jnp.concatenate([y[i * n : (i + 1) * n, n:] for i in range(k)], 1),
            ],
            0,
        )
        w = lmul(*left, z)
        return [(w[:n, i * n : (i + 1) * n], w[n:, i * n : (i + 1) * n]) for i in range(k)]

    dft = dict(left=(fc_hi, fc_lo), right=(f_hi, f_lo))
    inv = dict(left=(f_hi, f_lo), right=(fc_hi, fc_lo))
    prop = dict(left=(prop_ref[0], prop_ref[1]), right=(prop_ref[2], prop_ref[3]))
    adj = dict(left=(prop_ref[4], prop_ref[5]), right=(prop_ref[6], prop_ref[7]))

    local = q_refs[0].shape[0]
    order = [(c, k) for c in range(plan.cores) for k in range(local)]
    pairs = [order[i : i + 2] for i in range(0, len(order), 2)]

    def probe(c, k):
        return q_refs[c][k, 0].astype(F32), q_refs[c][k, 1].astype(F32)

    power = jnp.zeros((n, n), F32)
    at = 0
    for pair in pairs:
        parts = []
        for c, k in pair:
            qr, qi = probe(c, k)
            parts.append((qr * p1r - qi * p1i, qr * p1i + qi * p1r))
        waves = two_sided(parts, **prop)
        parts = []
        for i, (wr, wi) in enumerate(waves):
            wave_ref[at + i, 0] = wr
            wave_ref[at + i, 1] = wi
            parts.append((wr * p2r - wi * p2i, wr * p2i + wi * p2r))
        fars = two_sided(parts, **dft)
        for i, (fr, fi) in enumerate(fars):
            far_ref[at + i, 0] = fr
            far_ref[at + i, 1] = fi
            power += fr * fr + fi * fi
        at += len(pair)

    factor = 1.0 - amp_ref[slot].astype(F32) / jnp.maximum(jnp.sqrt(power), FLOOR)
    at = 0
    gsum_ref[...] = jnp.zeros_like(gsum_ref)
    for pair in pairs:
        parts = [(far_ref[at + i, 0] * factor, far_ref[at + i, 1] * factor) for i in range(len(pair))]
        backs = two_sided(parts, **inv)
        parts = []
        for i, (br, bi) in enumerate(backs):
            wr, wi = wave_ref[at + i, 0], wave_ref[at + i, 1]
            gsum_ref[3] += wr * br + wi * bi
            gsum_ref[4] += wr * bi - wi * br
            gsum_ref[5] += wr * wr + wi * wi
            parts.append((p2r * br + p2i * bi, p2r * bi - p2i * br))
        entries = two_sided(parts, **adj)
        for (er, ei), (c, k) in zip(entries, pair):
            qr, qi = probe(c, k)
            gsum_ref[0] += qr * er + qi * ei
            gsum_ref[1] += qr * ei - qi * er
            gsum_ref[2] += qr * qr + qi * qi
        at += len(pair)

    grads = gsum_ref.shape[0]
    for p in range(grads):
        g_out[p * n : (p + 1) * n, :] = jnp.where(live, gsum_ref[p], 0.0).astype(BF)

    def digits(shape, value):
        i = lax.broadcasted_iota(jnp.int32, shape, 0)
        high = lax.shift_right_logical(value, 4)
        low = value & 15
        return jnp.where(i == 0, high, jnp.where(i == 1, low, 0)).astype(F32).astype(BF)

    r_out = [onehot((m, n), lambda i, j, o=o: i + o == a + j) for o in row0]
    for z, r in zip(z_out, r_out):
        for p in range(grads):
            z[p * m : (p + 1) * m, :] = dot(r, g_out[p * n : (p + 1) * n, :]).astype(BF)
        z[grads * m :, :] = digits((TAIL, n), b)
    for c, x in enumerate(x_out):
        value = jnp.zeros((n, grads * m), F32)
        for p in range(grads):
            pick = onehot(
                (n, grads * m),
                lambda i, j, o=col0[c], p=p: (j >= p * m) & (j < (p + 1) * m) & (j - p * m + o == b + i),
            )
            value += dot(g_out[p * n : (p + 1) * n, :], pick)
        x[:n, :] = value.astype(BF)
        x[n:, :] = digits((TAIL, grads * m), a)
        for ph, r in enumerate(r_out):
            d_out[ph * n_col + c][...] = dot(r, x[:n, :]).astype(BF)


def final_kernel(plan, *refs):
    refs = list(refs)
    pos_ref, obj_ref = refs[:2]
    refs = refs[2:]
    n_row, n_col, cores = len(plan.rows), len(plan.cols), plan.cores

    def take(k):
        nonlocal refs
        head, refs = refs[:k], refs[k:]
        return head

    g_in = take(cores)
    z_in = [take(cores) for _ in range(n_row)]
    x_in = [take(cores) for _ in range(n_col)]
    d_in = [take(cores) for _ in range(n_row * n_col)]
    out_ref, u_ref, acc_ref = refs

    planes, block, side = obj_ref.shape
    n = g_in[0].shape[1]
    m = MARGIN
    grads = g_in[0].shape[0] // n
    step = pl.program_id(0)
    last = pl.num_programs(0) - 1
    me = lax.axis_index("probe")
    slots = [lax.rem(me + j, cores) for j in range(cores)]
    edge = -(-m // LANES) * LANES

    @pl.when(step == 0)
    def _():
        for j, g in enumerate(g_in):
            b = pos_ref[slots[j], 1]
            spread = onehot((n, side), lambda i, l: l + m == b + i)
            wide = dot(g[...], spread).astype(BF)
            for p in range(grads):
                u_ref[p, j * n : (j + 1) * n, :] = wide[p * n : (p + 1) * n, :]

    top = step * block + m
    rows = jnp.concatenate(
        [onehot((block, n), lambda i, w, j=j: i + top == pos_ref[slots[j], 0] + w) for j in range(cores)], 1
    )
    for p in range(grads):
        acc_ref[p] = dot(rows, u_ref[p])

    def decode(value):
        return (value[0:1, :].astype(F32) * 16.0 + value[1:2, :].astype(F32)).astype(jnp.int32)

    touched = []
    for ph in range(n_row):
        after = is_after("row", plan.rows[ph])
        touched.append(step == after * last)

        @pl.when(touched[ph])
        def _(ph=ph):
            spreads = []
            for z in z_in[ph]:
                b = decode(z[grads * m :, :])
                i = lax.broadcasted_iota(jnp.int32, (side, n), 0)
                w = lax.broadcasted_iota(jnp.int32, (side, n), 1)
                spreads.append(jnp.where(i + m == b + w, 1.0, 0.0).astype(BF))
            for p in range(grads):
                value = None
                for z, s in zip(z_in[ph], spreads):
                    term = lax.dot_general(
                        z[p * m : (p + 1) * m, :], s, (((1,), (1,)), ((), ())), preferred_element_type=F32
                    )
                    value = term if value is None else value + term
                acc_ref[p] += value

    for c in range(n_col):
        after = is_after("col", plan.cols[c])
        value = None
        for x in x_in[c]:
            a = decode(x[n:, :LANES])
            w = lax.broadcasted_iota(jnp.int32, (n, block), 0)
            i = lax.broadcasted_iota(jnp.int32, (n, block), 1)
            place = jnp.where(i + top == a[:, :block] + w, 1.0, 0.0).astype(BF)
            term = lax.dot_general(
                place, x[:n, :], (((0,), (0,)), ((), ())), preferred_element_type=F32
            )
            value = term if value is None else value + term
        for ph in range(n_row):
            both = None
            for d in d_in[ph * n_col + c]:
                term = d[...].astype(F32)
                both = term if both is None else both + term
            value += jnp.where(touched[ph], both, 0.0)
        hi, lo = split(value)
        lane0 = pl.multiple_of(after * (side - edge), LANES)
        offset = after * (edge - m)
        for p in range(grads):
            pick = onehot(
                (grads * m, edge),
                lambda i, l, p=p: (i >= p * m) & (i < (p + 1) * m) & (i - p * m + offset == l),
            )
            acc_ref[p, :, pl.ds(lane0, edge)] += dot(hi, pick) + dot(lo, pick)

    per = 3
    for s in range(grads // per):
        light = acc_ref[per * s + 2] + REGULAR
        for k in range(2):
            out_ref[2 * s + k] = obj_ref[2 * s + k].astype(F32) - acc_ref[per * s + k] / light


class Plan:
    def __init__(self, mesh):
        self.sizes = (mesh.shape["row"], mesh.shape["col"], mesh.shape["probe"])
        self.rows = phases_of(self.sizes[0])
        self.cols = phases_of(self.sizes[1])
        self.cores = self.sizes[2]

    def swap(self, value, row_phase, col_phase):
        return lax.ppermute(value, ("row", "col", "probe"), swap_pairs(self.sizes, row_phase, col_phase))

    def others(self, value):
        n = self.cores
        return [value] + [lax.ppermute(value, "probe", [((i + j) % n, i) for i in range(n)]) for j in range(1, n)]


def dft_pack(n):
    k = np.arange(n)
    phase = 2.0 * np.pi * ((k[:, None] * k[None, :]) % n) / n
    fr, fi = np.cos(phase) / np.sqrt(n), -np.sin(phase) / np.sqrt(n)
    return fr.astype(np.float32), fi.astype(np.float32)


def chirps(n, tilt_shift):
    u = jnp.arange(n, dtype=jnp.int32)
    u = (u + n // 2) % n - n // 2
    curve = ((u * u) % (4 * n)).astype(F32) / (4 * n)
    turns = tilt_shift[:, None] * u.astype(F32)[None, :] / n
    phase = (2.0 * np.pi) * (curve[None, :] + (turns - jnp.round(turns)))
    return jnp.stack([jnp.cos(phase), jnp.sin(phase)], 1).reshape(-1, n)


def body(plan, object_tiles, probe_modes, amplitudes, positions, counts, tilt_shift):
    slices, _, side, _ = object_tiles.shape
    planes = slices * 2
    n = probe_modes.shape[2]
    m = MARGIN
    grads = slices * 3
    slot_total = amplitudes.shape[2]
    assert slot_total == plan.cores
    obj = object_tiles.reshape(planes, side, side)
    pos = positions[0, 0]
    n_row, n_col = len(plan.rows), len(plan.cols)
    combos = [(r, c) for r in plan.rows for c in plan.cols]

    def sds(shape, dtype=BF):
        return jax.ShapeDtypeStruct(shape, dtype)

    strips = pl.pallas_call(
        functools.partial(prep_kernel, plan),
        out_shape=[sds((planes * m, side))] * n_row
        + [sds((side, planes * m))] * n_col
        + [sds((m, planes * m))] * len(combos),
        in_specs=[VMEM],
        out_specs=[VMEM] * (n_row + n_col + len(combos)),
        name="strips",
    )(obj)
    links = [(r, None) for r in plan.rows] + [(None, c) for c in plan.cols] + combos
    arrived = [plan.swap(v, *link) for v, link in zip(strips, links)]

    modes = plan.others(probe_modes)
    fr, fi = dft_pack(n)

    def np_split(x):
        hi = x.astype(jnp.bfloat16)
        return hi, (x - hi.astype(np.float32)).astype(jnp.bfloat16)

    fpack = np.block([[fr, fi], [-fi, fr]])
    fcpack = np.block([[fr, -fi], [fi, fr]])
    fpacks = jnp.asarray(np.stack([*np_split(fpack), *np_split(fcpack)]))
    props = pl.pallas_call(
        table_kernel,
        out_shape=sds((8, 2 * n, 2 * n)),
        in_specs=[VMEM, VMEM],
        out_specs=VMEM,
        name="tables",
        cost_estimate=pl.CostEstimate(flops=10**9, bytes_accessed=10**6, transcendentals=0),
    )(jnp.asarray(np.stack([fr, fi])), chirps(n, tilt_shift))

    modes_total = plan.cores * probe_modes.shape[0]
    msgs = pl.pallas_call(
        functools.partial(main_kernel, plan),
        out_shape=[sds((grads * m + TAIL, n))] * n_row
        + [sds((n + TAIL, grads * m))] * n_col
        + [sds((m, grads * m))] * len(combos)
        + [sds((grads * n, n))],
        in_specs=[SMEM, SMEM] + [VMEM] * (1 + len(links) + plan.cores + 3),
        out_specs=[VMEM] * (len(links) + 1),
        scratch_shapes=[
            pltpu.VMEM((modes_total, 2, n, n), F32),
            pltpu.VMEM((modes_total, 2, n, n), F32),
            pltpu.VMEM((grads, n, n), F32),
        ],
        name="waves",
    )(pos, counts, obj, *arrived, *modes, amplitudes[0, 0], fpacks, props)
    own = plan.others(msgs[-1])
    pieces = [plan.others(plan.swap(v, *link)) for v, link in zip(msgs[:-1], links)]
    flat = list(own) + [v for group in pieces for v in group]

    block = m
    const = lambda v: pl.BlockSpec(v.shape, lambda i: (0,) * v.ndim)
    updated = pl.pallas_call(
        functools.partial(final_kernel, plan),
        grid=(side // block,),
        out_shape=sds((planes, side, side), F32),
        in_specs=[SMEM, pl.BlockSpec((planes, block, side), lambda i: (0, i, 0))] + [const(v) for v in flat],
        out_specs=pl.BlockSpec((planes, block, side), lambda i: (0, i, 0)),
        scratch_shapes=[
            pltpu.VMEM((grads, plan.cores * n, side), BF),
            pltpu.VMEM((grads, block, side), F32),
        ],
        name="fold",
    )(pos, obj, *flat)
    return updated.reshape(object_tiles.shape)


def solution(mesh):
    plan = Plan(mesh)
    return jax.shard_map(
        functools.partial(body, plan),
        mesh=mesh,
        in_specs=(
            P("tilt", None, "row", "col"),
            P("probe", "tilt", None, None),
            P("row", "col", "tilt", None, None),
            P("row", "col", "tilt", None),
            P(("tilt", "row"), "col"),
            P("tilt"),
        ),
        out_specs=P("tilt", None, "row", "col"),
        check_vma=False,
    )
```

time: 271 us -> 60.7 us (0.22); the launches traced: 266 us -> 60.4 us
  matrix products: 72.9 us -> 0 us
  waiting for transfers between devices: 61.6 us -> 4.32 us
  local copies, waits for them, and re-layouts: 44.2 us -> 2.94 us
  Pallas kernels: 0 us -> 26.8 us
  other arithmetic: 26.4 us -> 0.79 us
  loops' own time: 15.7 us -> 0 us
  between operations: 13.9 us -> 0.88 us
  blocking collectives: 9.98 us -> 0 us
  starting transfers between devices: 21.1 us -> 24.7 us
    dot_general x96 -> x0, matrix products: 72.9 us -> none  [the longest x12 9.41 us: dft_pair(): jnp.einsum('mjl,lk->mjk', half_real, table_imag, precision=highest)]
    ppermute x8 -> x17, waiting for transfers between devices: 38 us -> 4.32 us  [the longest x10 3.05 us: swap(): lax.ppermute(value, ('row', 'col', 'probe'), swap_pairs(self.sizes, row_p...]
    pallas_call x0 -> x4, Pallas kernels: none -> 26.8 us  [the longest x1 12.5 us: body(): pl.pallas_call(functools.partial(main_kernel, plan), out_shape=[sds((grad...]
    psum x1 -> x0, waiting for transfers between devices: 23.6 us -> none  [body(): summed = lax.psum(folded.astype(jnp.bfloat16), 'probe').astype(jnp.float32)]
    another operation x1 -> x0, loops' own time: 15.7 us -> none  [body(): gradient = lax.fori_loop(0, slot_total, padded_step, zero_grad)]
    scatter-add x2 -> x0, local copies, waits for them, and re-layouts: 13.1 us -> none  [the longest x1 6.7 us: fold_cols(): return inner.at[:, :, :, -MARGIN:].add(arrived[:, :, :, -MARGIN:])]
    slice x12 -> x0, local copies, waits for them, and re-layouts: 11.2 us -> none  [the longest x1 5.15 us: fold_cols(): inner = gradient[:, :, :, MARGIN:-MARGIN]]
    psum x2 -> x0, blocking collectives: 9.98 us -> none  [padded_step(): lax.psum(local_power.astype(jnp.bfloat16), 'probe').astype(jnp.float32)]
  transfers between devices with their start and end apart: 9 -> 17, of which waited for: 9 -> 5; matrix products, arithmetic and copies ran while one was open for 3% -> 2% of each run, Pallas kernels for 0% -> 9%
where the time goes in v1:
time: 60.7 us; the launch traced here: 60.4 us
  Pallas kernels  26.8 us (44%)
  starting transfers between devices  24.7 us (41%)
  waiting for transfers between devices  4.32 us (7%)
  local copies, waits for them, and re-layouts  2.94 us (5%)
  between operations  0.88 us (1%)
  other arithmetic  0.79 us (1%)
    ppermute x10, starting transfers between devices, swap(): lax.ppermute(value, ('row', 'col', 'probe'), swap_pairs(self.sizes, row_p...  18 us
    pallas_call x1, Pallas kernels, body(): pl.pallas_call(functools.partial(main_kernel, plan), out_shape=[sds((grad...  12.5 us
    pallas_call x1, Pallas kernels, body(): pl.pallas_call(functools.partial(final_kernel, plan), grid=(side // block...  9.17 us
    ppermute x7, starting transfers between devices, others(): lax.ppermute(value, 'probe', [((i + j) % n, i) for i in range(n)])  6.68 us
    ppermute x10, waiting for transfers between devices, swap(): lax.ppermute(value, ('row', 'col', 'probe'), swap_pairs(self.sizes, row_p...  3.05 us
    pallas_call x1, Pallas kernels, body(): pl.pallas_call(functools.partial(prep_kernel, plan), out_shape=[sds((plan...  2.61 us
    pallas_call x1, Pallas kernels, body(): pl.pallas_call(table_kernel, out_shape=sds((8, 2 * n, 2 * n)), in_specs=[...  2.53 us
    unnamed x34, local copies, waits for them, and re-layouts  2.36 us
  transfers between devices with their start and end apart: 17, of which 5 were waited for; matrix products, arithmetic and copies ran while one was open for 2% of the time, Pallas kernels for 9%

profile of v1, /device:TPU:13, one launch (start us, length us, event | category | flops | bytes accessed | tf_op | source)
XLA Modules:
  0.0 60.4 jit_solution(18389881718733477517)
XLA Ops:
  0.0 0.7 %collective-permute-start.5 = (bf16[4,2,128,128]{3,2,1,0:T(8,128)(2,1)}, bf16[4,2,128,128]{3,2,1,0:T(8,128)(2,1)S(1)}, u32[]{:S(2)}, u32[]{:S(2)}) collective-permute-start(bf16[4,2,128,128]{3,2,1,0:T(8,128)(2,1)} %refs_8_.1), channel_id=1, source_target_pairs={{1,0},{0,1},{3,2},{2,3},{5,4},{4,5},{7,6},{6,7},{9,8},{8,9},{11,10... | collective-permute-start | bytes 786440 | tf_op jit(solution)/shard_map/ppermute | solution.py:399
  0.7 2.6 %strips.1 = (bf16[384,384]{1,0:T(8,128)(2,1)}, bf16[384,384]{1,0:T(8,128)(2,1)}, bf16[384,384]{1,0:T(8,128)(2,1)}, bf16[96,384]{1,0:T(8,128)(2,1)}, bf16[96,384]{1,0:T(8,128)(2,1)}) custom-call(bf16[4,384,384]{2,1,0:T(8,128)(2,1)} %bitcast.5), custom_call_target="tpu_custom_call" | custom-call | tf_op jit(solution)/shard_map/strips/pallas_call | solution.py:434
  3.3 1.1 %collective-permute-start.3 = (bf16[96,384]{1,0:T(8,128)(2,1)}, bf16[96,384]{1,0:T(8,128)(2,1)S(1)}, u32[]{:S(2)}, u32[]{:S(2)}) collective-permute-start(bf16[96,384]{1,0:T(8,128)(2,1)} %get-tuple-element.19), channel_id=1, source_target_pairs={{0,6},{1,7},{2,4},{3,5},{4,2},{5,3},{6,0},{7,1},{8,14},{9,15},{10,... | collective-permute-start | bytes 221192 | tf_op jit(solution)/shard_map/ppermute | solution.py:395
  4.4 1.3 %collective-permute-start = (bf16[384,384]{1,0:T(8,128)(2,1)}, bf16[384,384]{1,0:T(8,128)(2,1)S(1)}, u32[]{:S(2)}, u32[]{:S(2)}) collective-permute-start(bf16[384,384]{1,0:T(8,128)(2,1)} %get-tuple-element.16), channel_id=1, source_target_pairs={{0,4},{1,5},{2,6},{3,7},{4,0},{5,1},{6,2},{7,3},{8,12},{9,13},{10,... | collective-permute-start | bytes 884744 | tf_op jit(solution)/shard_map/ppermute | solution.py:395
  5.7 3.2 %collective-permute-start.1 = (bf16[384,384]{1,0:T(8,128)(2,1)}, bf16[384,384]{1,0:T(8,128)(2,1)S(1)}, u32[]{:S(2)}, u32[]{:S(2)}) collective-permute-start(bf16[384,384]{1,0:T(8,128)(2,1)} %get-tuple-element.17), channel_id=1, source_target_pairs={{4,8},{5,9},{6,10},{7,11},{8,4},{9,5},{10,6},{11,7},{20,24},{21,25... | collective-permute-start | bytes 884744 | tf_op jit(solution)/shard_map/ppermute | solution.py:395
  9.2 0.8 %fusion.9 = (f32[2,1,128]{2,0,1:T(2,128)S(1)}, f32[2,1,128]{2,0,1:T(2,128)S(1)}) fusion(f32[128]{0:T(128)S(1)} %fusion.7, f32[2]{0:T(128)} %param.13, f32[128]{0:T(128)S(1)} %fusion.4), kind=kLoop, calls=%fused_computation.17 | loop fusion | flops 1536 | bytes 3080 | tf_op jit(solution)/shard_map/cos | solution.py:415
  10.7 0.6 copy.9
  11.2 3.0 %collective-permute-start.4 = (bf16[96,384]{1,0:T(8,128)(2,1)}, bf16[96,384]{1,0:T(8,128)(2,1)S(1)}, u32[]{:S(2)}, u32[]{:S(2)}) collective-permute-start(bf16[96,384]{1,0:T(8,128)(2,1)} %get-tuple-element.20), channel_id=1, source_target_pairs={{4,10},{5,11},{6,8},{7,9},{8,6},{9,7},{10,4},{11,5},{20,26},{21,27... | collective-permute-start | bytes 221192 | tf_op jit(solution)/shard_map/ppermute | solution.py:395
  14.2 2.5 %tables.1.refs_12_ = bf16[8,256,256]{2,1,0:T(8,128)(2,1)} custom-call(f32[2,128,128]{2,1,0:T(8,128)} %constant.43.clone.f_ref, f32[4,128]{1,0:T(4,128)} %bitcast.11), custom_call_target="tpu_custom_call" | custom-call | flops 1000000000 | bytes 1000000 | tf_op jit(solution)/shard_map/tables/pallas_call | solution.py:456
  16.8 0.8 %collective-permute-done.4.refs_7_ = bf16[96,384]{1,0:T(8,128)(2,1)S(1)} collective-permute-done((bf16[96,384]{1,0:T(8,128)(2,1)}, bf16[96,384]{1,0:T(8,128)(2,1)S(1)}, u32[]{:S(2)}, u32[]{:S(2)}) %collective-permute-start.4) | collective-permute-done | bytes 73760 | tf_op jit(solution)/shard_map/ppermute | solution.py:395
  17.6 0.6 copy-done.16
  18.6 12.5 %waves.1 = (bf16[592,128]{1,0:T(8,128)(2,1)}, bf16[592,128]{1,0:T(8,128)(2,1)}, bf16[144,576]{1,0:T(8,128)(2,1)}, bf16[96,576]{1,0:T(8,128)(2,1)}, bf16[96,576]{1,0:T(8,128)(2,1)}, /*index=5*/bf16[768,128]{1,0:T(8,128)(2,1)}) custom-call(s32[2,2]{1,0:T(2,128)} %bitcast.9, s32[1,1]{1,0:T(1,128)S(6)} %copy.10.refs_1_, bf16[4,384,384]{2,1,0:T(8,128)(2,1)} %bitcast.6, ...), custom_call_target="tpu_custom_call" | custom-call | tf_op jit(solution)/shard_map/waves/pallas_call | solution.py:466
  31.1 1.3 %collective-permute-start.11 = (bf16[144,576]{1,0:T(8,128)(2,1)}, bf16[144,576]{1,0:T(8,128)(2,1)S(1)}, u32[]{:S(2)}, u32[]{:S(2)}) collective-permute-start(bf16[144,576]{1,0:T(8,128)(2,1)} %get-tuple-element.24), channel_id=1, source_target_pairs={{0,2},{1,3},{2,0},{3,1},{4,6},{5,7},{6,4},{7,5},{8,10},{9,11},{10,... | collective-permute-start | bytes 497672 | tf_op jit(solution)/shard_map/ppermute | solution.py:395
  32.4 2.5 %collective-permute-start.6 = (bf16[768,128]{1,0:T(8,128)(2,1)}, bf16[768,128]{1,0:T(8,128)(2,1)S(1)}, u32[]{:S(2)}, u32[]{:S(2)}) collective-permute-start(bf16[768,128]{1,0:T(8,128)(2,1)} %get-tuple-element.21.refs_2_), channel_id=1, source_target_pairs={{1,0},{0,1},{3,2},{2,3},{5,4},{4,5},{7,6},{6,7},{9,8},{8,9},{11,10... | collective-permute-start | bytes 589832 | tf_op jit(solution)/shard_map/ppermute | solution.py:399
  34.8 1.8 %collective-permute-start.7 = (bf16[592,128]{1,0:T(8,128)(2,1)}, bf16[592,128]{1,0:T(8,128)(2,1)S(1)}, u32[]{:S(2)}, u32[]{:S(2)}) collective-permute-start(bf16[592,128]{1,0:T(8,128)(2,1)} %get-tuple-element.22), channel_id=1, source_target_pairs={{0,4},{1,5},{2,6},{3,7},{4,0},{5,1},{6,2},{7,3},{8,12},{9,13},{10,... | collective-permute-start | bytes 454664 | tf_op jit(solution)/shard_map/ppermute | solution.py:395
  36.6 2.2 %collective-permute-start.9 = (bf16[592,128]{1,0:T(8,128)(2,1)}, bf16[592,128]{1,0:T(8,128)(2,1)S(1)}, u32[]{:S(2)}, u32[]{:S(2)}) collective-permute-start(bf16[592,128]{1,0:T(8,128)(2,1)} %get-tuple-element.23), channel_id=1, source_target_pairs={{4,8},{5,9},{6,10},{7,11},{8,4},{9,5},{10,6},{11,7},{20,24},{21,25... | collective-permute-start | bytes 454664 | tf_op jit(solution)/shard_map/ppermute | solution.py:395
  38.8 3.9 %collective-permute-start.15 = (bf16[96,576]{1,0:T(8,128)(2,1)}, bf16[96,576]{1,0:T(8,128)(2,1)S(1)}, u32[]{:S(2)}, u32[]{:S(2)}) collective-permute-start(bf16[96,576]{1,0:T(8,128)(2,1)} %get-tuple-element.26), channel_id=1, source_target_pairs={{4,10},{5,11},{6,8},{7,9},{8,6},{9,7},{10,4},{11,5},{20,26},{21,27... | collective-permute-start | bytes 331784 | tf_op jit(solution)/shard_map/ppermute | solution.py:395
  42.7 0.9 %collective-permute-start.12 = (bf16[144,576]{1,0:T(8,128)(2,1)S(1)}, bf16[144,576]{1,0:T(8,128)(2,1)S(1)}, u32[]{:S(2)}, u32[]{:S(2)}) collective-permute-start(bf16[144,576]{1,0:T(8,128)(2,1)S(1)} %collective-permute-done.11.refs_8_), channel_id=1, source_target_pairs={{1,0},{0,1},{3,2},{2,3},{5,4},{4,5},{7,6},{6,7},{9,8},{8,9},{11,10... | collective-permute-start | bytes 497672 | tf_op jit(solution)/shard_map/ppermute | solution.py:399
  43.9 1.3 %collective-permute-start.10 = (bf16[592,128]{1,0:T(8,128)(2,1)S(1)}, bf16[592,128]{1,0:T(8,128)(2,1)S(1)}, u32[]{:S(2)}, u32[]{:S(2)}) collective-permute-start(bf16[592,128]{1,0:T(8,128)(2,1)S(1)} %collective-permute-done.9.refs_6_), channel_id=1, source_target_pairs={{1,0},{0,1},{3,2},{2,3},{5,4},{4,5},{7,6},{6,7},{9,8},{8,9},{11,10... | collective-permute-start | bytes 454664 | tf_op jit(solution)/shard_map/ppermute | solution.py:399
  45.2 2.1 %collective-permute-done.15.refs_12_ = bf16[96,576]{1,0:T(8,128)(2,1)S(1)} collective-permute-done((bf16[96,576]{1,0:T(8,128)(2,1)}, bf16[96,576]{1,0:T(8,128)(2,1)S(1)}, u32[]{:S(2)}, u32[]{:S(2)}) %collective-permute-start.15) | collective-permute-done | bytes 110624 | tf_op jit(solution)/shard_map/ppermute | solution.py:395
  47.3 1.1 %collective-permute-start.14 = (bf16[96,576]{1,0:T(8,128)(2,1)S(1)}, bf16[96,576]{1,0:T(8,128)(2,1)S(1)}, u32[]{:S(2)}, u32[]{:S(2)}) collective-permute-start(bf16[96,576]{1,0:T(8,128)(2,1)S(1)} %collective-permute-done.13.refs_10_), channel_id=1, source_target_pairs={{1,0},{0,1},{3,2},{2,3},{5,4},{4,5},{7,6},{6,7},{9,8},{8,9},{11,10... | collective-permute-start | bytes 331784 | tf_op jit(solution)/shard_map/ppermute | solution.py:399
  48.5 0.9 %collective-permute-done.14.refs_11_ = bf16[96,576]{1,0:T(8,128)(2,1)S(1)} collective-permute-done((bf16[96,576]{1,0:T(8,128)(2,1)S(1)}, bf16[96,576]{1,0:T(8,128)(2,1)S(1)}, u32[]{:S(2)}, u32[]{:S(2)}) %collective-permute-start.14) | collective-permute-done | bytes 110624 | tf_op jit(solution)/shard_map/ppermute | solution.py:399
  50.6 0.7 %copy-done.6 = bf16[144,576]{1,0:T(8,128)(2,1)} copy-done((bf16[144,576]{1,0:T(8,128)(2,1)}, bf16[144,576]{1,0:T(8,128)(2,1)S(1)}, u32[]{:S(2)}) %copy-start.6) | copy-done | bytes 165912
  51.3 9.2 %fold.1 = f32[4,384,384]{2,1,0:T(8,128)} custom-call(s32[2,2]{1,0:T(2,128)} %bitcast.10, bf16[4,384,384]{2,1,0:T(8,128)(2,1)} %bitcast.7, bf16[768,128]{1,0:T(8,128)(2,1)} %get-tuple-element.21.refs_2_, bf16[768,128]{1,0:T(8,128)(2,1)} %copy-done.4, bf16[592,128]{1,0:T(8,128)(2,1)} %copy-done.7, bf16[592,128]{1,0:T(8,128)(2,1)} %copy-done.9, ...), custom_call_target="tpu_custom_call" | custom-call | tf_op jit(solution)/shard_map/fold/pallas_call | solution.py:487
  (53 shorter events, 2.2 us)
Async XLA Ops:
  0.0 17.5 %collective-permute-start.5 = (bf16[4,2,128,128]{3,2,1,0:T(8,128)(2,1)}, bf16[4,2,128,128]{3,2,1,0:T(8,128)(2,1)S(1)}, u32[]{:S(2)}, u32[]{:S(2)}) collective-permute-start(bf16[4,2,128,128]{3,2,1,0:T(8,128)(2,1)} %refs_8_.1), channel_id=1, source_target_pairs={{1,0},{0,1},{3,2},{2,3},{5,4},{4,5},{7,6},{6,7},{9,8},{8,9},{11,10... | collective-permute-start | bytes 786440 | tf_op jit(solution)/shard_map/ppermute | solution.py:399
  3.3 7.9 %collective-permute-start.3 = (bf16[96,384]{1,0:T(8,128)(2,1)}, bf16[96,384]{1,0:T(8,128)(2,1)S(1)}, u32[]{:S(2)}, u32[]{:S(2)}) collective-permute-start(bf16[96,384]{1,0:T(8,128)(2,1)} %get-tuple-element.19), channel_id=1, source_target_pairs={{0,6},{1,7},{2,4},{3,5},{4,2},{5,3},{6,0},{7,1},{8,14},{9,15},{10,... | collective-permute-start | bytes 221192 | tf_op jit(solution)/shard_map/ppermute | solution.py:395
  4.4 13.2 %collective-permute-start = (bf16[384,384]{1,0:T(8,128)(2,1)}, bf16[384,384]{1,0:T(8,128)(2,1)S(1)}, u32[]{:S(2)}, u32[]{:S(2)}) collective-permute-start(bf16[384,384]{1,0:T(8,128)(2,1)} %get-tuple-element.16), channel_id=1, source_target_pairs={{0,4},{1,5},{2,6},{3,7},{4,0},{5,1},{6,2},{7,3},{8,12},{9,13},{10,... | collective-permute-start | bytes 884744 | tf_op jit(solution)/shard_map/ppermute | solution.py:395
  5.7 11.9 %collective-permute-start.1 = (bf16[384,384]{1,0:T(8,128)(2,1)}, bf16[384,384]{1,0:T(8,128)(2,1)S(1)}, u32[]{:S(2)}, u32[]{:S(2)}) collective-permute-start(bf16[384,384]{1,0:T(8,128)(2,1)} %get-tuple-element.17), channel_id=1, source_target_pairs={{4,8},{5,9},{6,10},{7,11},{8,4},{9,5},{10,6},{11,7},{20,24},{21,25... | collective-permute-start | bytes 884744 | tf_op jit(solution)/shard_map/ppermute | solution.py:395
  8.9 8.7 %collective-permute-start.2 = (bf16[384,384]{1,0:T(8,128)(2,1)}, bf16[384,384]{1,0:T(8,128)(2,1)S(1)}, u32[]{:S(2)}, u32[]{:S(2)}) collective-permute-start(bf16[384,384]{1,0:T(8,128)(2,1)} %get-tuple-element.18), channel_id=1, source_target_pairs={{0,2},{1,3},{2,0},{3,1},{4,6},{5,7},{6,4},{7,5},{8,10},{9,11},{10,... | collective-permute-start | bytes 884744 | tf_op jit(solution)/shard_map/ppermute | solution.py:395
  11.2 6.4 %copy-start.15 = (bf16[96,384]{1,0:T(8,128)(2,1)}, bf16[96,384]{1,0:T(8,128)(2,1)S(1)}, u32[]{:S(2)}) copy-start(bf16[96,384]{1,0:T(8,128)(2,1)S(1)} %collective-permute-done.3.refs_6_) | copy-start | bytes 221188
  11.2 6.3 %collective-permute-start.4 = (bf16[96,384]{1,0:T(8,128)(2,1)}, bf16[96,384]{1,0:T(8,128)(2,1)S(1)}, u32[]{:S(2)}, u32[]{:S(2)}) collective-permute-start(bf16[96,384]{1,0:T(8,128)(2,1)} %get-tuple-element.20), channel_id=1, source_target_pairs={{4,10},{5,11},{6,8},{7,9},{8,6},{9,7},{10,4},{11,5},{20,26},{21,27... | collective-permute-start | bytes 221192 | tf_op jit(solution)/shard_map/ppermute | solution.py:395
  31.1 7.7 %collective-permute-start.13 = (bf16[96,576]{1,0:T(8,128)(2,1)}, bf16[96,576]{1,0:T(8,128)(2,1)S(1)}, u32[]{:S(2)}, u32[]{:S(2)}) collective-permute-start(bf16[96,576]{1,0:T(8,128)(2,1)} %get-tuple-element.25), channel_id=1, source_target_pairs={{0,6},{1,7},{2,4},{3,5},{4,2},{5,3},{6,0},{7,1},{8,14},{9,15},{10,... | collective-permute-start | bytes 331784 | tf_op jit(solution)/shard_map/ppermute | solution.py:395
  31.1 11.6 %collective-permute-start.11 = (bf16[144,576]{1,0:T(8,128)(2,1)}, bf16[144,576]{1,0:T(8,128)(2,1)S(1)}, u32[]{:S(2)}, u32[]{:S(2)}) collective-permute-start(bf16[144,576]{1,0:T(8,128)(2,1)} %get-tuple-element.24), channel_id=1, source_target_pairs={{0,2},{1,3},{2,0},{3,1},{4,6},{5,7},{6,4},{7,5},{8,10},{9,11},{10,... | collective-permute-start | bytes 497672 | tf_op jit(solution)/shard_map/ppermute | solution.py:395
  32.4 16.1 %collective-permute-start.6 = (bf16[768,128]{1,0:T(8,128)(2,1)}, bf16[768,128]{1,0:T(8,128)(2,1)S(1)}, u32[]{:S(2)}, u32[]{:S(2)}) collective-permute-start(bf16[768,128]{1,0:T(8,128)(2,1)} %get-tuple-element.21.refs_2_), channel_id=1, source_target_pairs={{1,0},{0,1},{3,2},{2,3},{5,4},{4,5},{7,6},{6,7},{9,8},{8,9},{11,10... | collective-permute-start | bytes 589832 | tf_op jit(solution)/shard_map/ppermute | solution.py:399
  34.8 8.8 %collective-permute-start.7 = (bf16[592,128]{1,0:T(8,128)(2,1)}, bf16[592,128]{1,0:T(8,128)(2,1)S(1)}, u32[]{:S(2)}, u32[]{:S(2)}) collective-permute-start(bf16[592,128]{1,0:T(8,128)(2,1)} %get-tuple-element.22), channel_id=1, source_target_pairs={{0,4},{1,5},{2,6},{3,7},{4,0},{5,1},{6,2},{7,3},{8,12},{9,13},{10,... | collective-permute-start | bytes 454664 | tf_op jit(solution)/shard_map/ppermute | solution.py:395
  36.6 7.3 %collective-permute-start.9 = (bf16[592,128]{1,0:T(8,128)(2,1)}, bf16[592,128]{1,0:T(8,128)(2,1)S(1)}, u32[]{:S(2)}, u32[]{:S(2)}) collective-permute-start(bf16[592,128]{1,0:T(8,128)(2,1)} %get-tuple-element.23), channel_id=1, source_target_pairs={{4,8},{5,9},{6,10},{7,11},{8,4},{9,5},{10,6},{11,7},{20,24},{21,25... | collective-permute-start | bytes 454664 | tf_op jit(solution)/shard_map/ppermute | solution.py:395
  38.8 11.0 %copy-start.11 = (bf16[96,576]{1,0:T(8,128)(2,1)}, bf16[96,576]{1,0:T(8,128)(2,1)S(1)}, u32[]{:S(2)}) copy-start(bf16[96,576]{1,0:T(8,128)(2,1)S(1)} %collective-permute-done.13.refs_10_) | copy-start | bytes 331780
  38.8 8.5 %collective-permute-start.15 = (bf16[96,576]{1,0:T(8,128)(2,1)}, bf16[96,576]{1,0:T(8,128)(2,1)S(1)}, u32[]{:S(2)}, u32[]{:S(2)}) collective-permute-start(bf16[96,576]{1,0:T(8,128)(2,1)} %get-tuple-element.26), channel_id=1, source_target_pairs={{4,10},{5,11},{6,8},{7,9},{8,6},{9,7},{10,4},{11,5},{20,26},{21,27... | collective-permute-start | bytes 331784 | tf_op jit(solution)/shard_map/ppermute | solution.py:395
  42.7 7.2 %copy-start.5 = (bf16[144,576]{1,0:T(8,128)(2,1)}, bf16[144,576]{1,0:T(8,128)(2,1)S(1)}, u32[]{:S(2)}) copy-start(bf16[144,576]{1,0:T(8,128)(2,1)S(1)} %collective-permute-done.11.refs_8_) | copy-start | bytes 497668
  42.7 7.1 %collective-permute-start.12 = (bf16[144,576]{1,0:T(8,128)(2,1)S(1)}, bf16[144,576]{1,0:T(8,128)(2,1)S(1)}, u32[]{:S(2)}, u32[]{:S(2)}) collective-permute-start(bf16[144,576]{1,0:T(8,128)(2,1)S(1)} %collective-permute-done.11.refs_8_), channel_id=1, source_target_pairs={{1,0},{0,1},{3,2},{2,3},{5,4},{4,5},{7,6},{6,7},{9,8},{8,9},{11,10... | collective-permute-start | bytes 497672 | tf_op jit(solution)/shard_map/ppermute | solution.py:399
  43.6 6.2 %copy-start.7 = (bf16[592,128]{1,0:T(8,128)(2,1)}, bf16[592,128]{1,0:T(8,128)(2,1)S(1)}, u32[]{:S(2)}) copy-start(bf16[592,128]{1,0:T(8,128)(2,1)S(1)} %collective-permute-done.7.refs_4_) | copy-start | bytes 454660
  43.6 6.2 %collective-permute-start.8 = (bf16[592,128]{1,0:T(8,128)(2,1)S(1)}, bf16[592,128]{1,0:T(8,128)(2,1)S(1)}, u32[]{:S(2)}, u32[]{:S(2)}) collective-permute-start(bf16[592,128]{1,0:T(8,128)(2,1)S(1)} %collective-permute-done.7.refs_4_), channel_id=1, source_target_pairs={{1,0},{0,1},{3,2},{2,3},{5,4},{4,5},{7,6},{6,7},{9,8},{8,9},{11,10... | collective-permute-start | bytes 454664 | tf_op jit(solution)/shard_map/ppermute | solution.py:399
  43.9 6.0 %copy-start.8 = (bf16[592,128]{1,0:T(8,128)(2,1)}, bf16[592,128]{1,0:T(8,128)(2,1)S(1)}, u32[]{:S(2)}) copy-start(bf16[592,128]{1,0:T(8,128)(2,1)S(1)} %collective-permute-done.9.refs_6_) | copy-start | bytes 454660
  43.9 5.9 %collective-permute-start.10 = (bf16[592,128]{1,0:T(8,128)(2,1)S(1)}, bf16[592,128]{1,0:T(8,128)(2,1)S(1)}, u32[]{:S(2)}, u32[]{:S(2)}) collective-permute-start(bf16[592,128]{1,0:T(8,128)(2,1)S(1)} %collective-permute-done.9.refs_6_), channel_id=1, source_target_pairs={{1,0},{0,1},{3,2},{2,3},{5,4},{4,5},{7,6},{6,7},{9,8},{8,9},{11,10... | collective-permute-start | bytes 454664 | tf_op jit(solution)/shard_map/ppermute | solution.py:399
  47.3 2.6 %copy-start.12 = (bf16[96,576]{1,0:T(8,128)(2,1)}, bf16[96,576]{1,0:T(8,128)(2,1)S(1)}, u32[]{:S(2)}) copy-start(bf16[96,576]{1,0:T(8,128)(2,1)S(1)} %collective-permute-done.15.refs_12_) | copy-start | bytes 331780
  47.3 2.1 %collective-permute-start.14 = (bf16[96,576]{1,0:T(8,128)(2,1)S(1)}, bf16[96,576]{1,0:T(8,128)(2,1)S(1)}, u32[]{:S(2)}, u32[]{:S(2)}) collective-permute-start(bf16[96,576]{1,0:T(8,128)(2,1)S(1)} %collective-permute-done.13.refs_10_), channel_id=1, source_target_pairs={{1,0},{0,1},{3,2},{2,3},{5,4},{4,5},{7,6},{6,7},{9,8},{8,9},{11,10... | collective-permute-start | bytes 331784 | tf_op jit(solution)/shard_map/ppermute | solution.py:399
  48.5 1.4 %copy-start.4 = (bf16[768,128]{1,0:T(8,128)(2,1)}, bf16[768,128]{1,0:T(8,128)(2,1)S(1)}, u32[]{:S(2)}) copy-start(bf16[768,128]{1,0:T(8,128)(2,1)S(1)} %collective-permute-done.6.refs_3_) | copy-start | bytes 589828
  48.5 1.3 %collective-permute-start.16 = (bf16[96,576]{1,0:T(8,128)(2,1)S(1)}, bf16[96,576]{1,0:T(8,128)(2,1)S(1)}, u32[]{:S(2)}, u32[]{:S(2)}) collective-permute-start(bf16[96,576]{1,0:T(8,128)(2,1)S(1)} %collective-permute-done.15.refs_12_), channel_id=1, source_target_pairs={{1,0},{0,1},{3,2},{2,3},{5,4},{4,5},{7,6},{6,7},{9,8},{8,9},{11,10... | collective-permute-start | bytes 331784 | tf_op jit(solution)/shard_map/ppermute | solution.py:399
  (10 other events, 7.5 us)
